TPU v7x, 256 devices: a whole 4x4x8 slice. The times are simulated.
256 devices in a mesh: band: 4 (over x), tile: 64 (over y, z, core).
Axes of the slice: x: 4, y: 4, z: 8, core: 2. Of those that a mesh axis runs over, the one named last changes fastest.
Arguments:
- granules: bfloat16 [1024, 16, 4096], P('tile', 'band'), may hold values from -6 to 6
- valid_rows: int32 [1024, 64], P('tile'), may hold values 0 or 1
- scene_order: int32 [1024], P('tile'), may hold values from 0 to 1023, each once
- intersections: int32 [1024, 4], P('tile'), may hold values from 0 to 63, all different within a row; in each aligned block of 16 rows (0 to 15, 16 to 31, ...) at most 2 rows name the same one
- row_resample: bfloat16 [1024, 4, 4096], P('tile'), may hold values from 0 to 1.4, as said below
- col_resample: bfloat16 [1024, 4, 4096], P('tile'), may hold values from 0 to 1.4, as said below
- w_in: bfloat16 [16, 256], replicated, may hold values from -1.5 to 1.5
- w_hidden: bfloat16 [2, 256, 256], replicated, may hold values from -0.375 to 0.375
- w_out: bfloat16 [256], replicated, may hold values from -1.5 to 1.5
Outputs:
- composite: float32 [16, 262144], P('band', 'tile')
Inputs may be any that keep to these rules, and one draw needn't show every extreme that they name: `intersections`: each scene names 4 different output tiles; the 16 scenes of one device name any one tile at most 2 times, a bound that some block reaches. `scene_order`: each order number appears once. `row_resample`: nonnegative resampling weights. `col_resample`: nonnegative resampling weights.
All inputs are finite; a program needn't handle non-finite values. No bound on the sum of `valid_rows` on one device may be relied on, other than what follows from the above.
Results may differ from a plain program's by a relative error of at most 0.0031.
Values may be sent and summed in bfloat16 or wider, within the bound.
No kernel may reach another device: no remote copies, remote signals or barrier semaphores. Data moves between devices by JAX's collectives and lax.ppermute only.
A program may use at most 128 MiB of HBM per device.

v0:
```python
import jax
import jax.numpy as jnp
from jax import lax
from jax.sharding import PartitionSpec as P

HUBER_ITERS = 4
SMOOTH = 2
prior_weight = 0.25
huber_delta = 0.5
edge_scale = 1.0
smooth_rate = 0.2


def extended_2(block, sides, width):
    for axis, dim in sides:
        count = lax.axis_size(axis)
        forward = [(i, i + 1) for i in range(count - 1)]
        backward = [(target, source) for source, target in forward]
        low = lax.ppermute(
            lax.slice_in_dim(block, block.shape[dim] - width, None, axis=dim), axis, forward
        )
        high = lax.ppermute(lax.slice_in_dim(block, 0, width, axis=dim), axis, backward)
        block = jnp.concatenate([low, block, high], axis=dim)
    return block


def scene_weights(pixels, valid_part, recency, w_in, w_hidden, w_out, side_cells):
    scenes, row_count = valid_part.shape
    valid_pix = jnp.broadcast_to(
        valid_part.astype(jnp.float32)[:, :, None], (scenes, row_count, side_cells)
    )
    valid_pix = valid_pix.reshape(scenes, row_count * side_cells)

    def one_scene(inputs):
        scene_pixels, scene_valid, scene_recency = inputs
        hidden = jax.nn.silu(
            jnp.einsum("cn,ch->nh", scene_pixels, w_in, preferred_element_type=jnp.float32)
        ).astype(jnp.bfloat16)
        for repeat in range(w_hidden.shape[0]):
            hidden = jax.nn.silu(
                jnp.dot(hidden, w_hidden[repeat], preferred_element_type=jnp.float32)
            ).astype(jnp.bfloat16)
        logits = jnp.dot(hidden, w_out, preferred_element_type=jnp.float32)
        return (jax.nn.sigmoid(-logits) * scene_valid * scene_recency).astype(jnp.bfloat16)

    return lax.map(one_scene, (pixels, valid_pix, recency))


def reproject(planes, rows_matrix, cols_matrix):
    half_done = jnp.einsum(
        "ncil,njl->ncij", planes, cols_matrix, preferred_element_type=jnp.float32
    ).astype(jnp.bfloat16)
    return jnp.einsum(
        "nij,ncjl->ncil", rows_matrix, half_done, preferred_element_type=jnp.float32
    ).astype(jnp.bfloat16)


def huber_merge(observed, weights):
    values = observed.astype(jnp.float32)
    plain = weights.astype(jnp.float32)[:, None, :]
    estimate = jnp.sum(plain * values, 0) / (jnp.sum(plain, 0) + prior_weight)
    for repeat in range(HUBER_ITERS):
        residual = values - estimate[None]
        huber_w = plain * huber_delta / jnp.maximum(jnp.abs(residual), huber_delta)
        estimate = jnp.sum(huber_w * values, 0) / (jnp.sum(huber_w, 0) + prior_weight)
    return estimate


def smooth_step(extended, first_col, total_cols):
    positions = first_col + jnp.arange(extended.shape[2] - 1)
    inside = ((positions >= 0) & (positions + 1 < total_cols)).astype(jnp.float32)
    across = extended[:, :, 1:] - extended[:, :, :-1]
    sideways = across / (1.0 + (across / edge_scale) ** 2) * inside
    centre = extended[:, :, 1:-1]
    upward_diff = centre[:, 1:, :] - centre[:, :-1, :]
    upward = upward_diff / (1.0 + (upward_diff / edge_scale) ** 2)
    zeros_row = jnp.zeros_like(upward[:, :1, :])
    vertical = jnp.concatenate([upward, zeros_row], 1) - jnp.concatenate([zeros_row, upward], 1)
    return centre + smooth_rate * (sideways[:, :, 1:] - sideways[:, :, :-1] + vertical)


def per_device(
    granules,
    valid_rows,
    scene_order,
    intersections,
    row_resample,
    col_resample,
    w_in,
    w_hidden,
    w_out,
):
    scenes, group_bands, pixel_count = granules.shape
    side_cells = valid_rows.shape[1]
    intersection_count = intersections.shape[1]
    tile_count = lax.axis_size("tile")
    band_count = lax.axis_size("band")
    recency = jnp.exp(1.4 * scene_order.astype(jnp.float32) / (scenes * tile_count) - 0.7)
    by_rows = lax.all_to_all(granules, "band", split_axis=2, concat_axis=1, tiled=True)
    row_count = side_cells // band_count
    valid_here = lax.dynamic_slice_in_dim(
        valid_rows, lax.axis_index("band") * row_count, row_count, 1
    )
    partial_weights = scene_weights(by_rows, valid_here, recency, w_in, w_hidden, w_out, side_cells)
    weights = lax.all_gather(partial_weights, "band", axis=1, tiled=True)
    plane_count = group_bands + 1
    planes = jnp.concatenate([granules, weights[:, None, :]], 1)
    entry_count = scenes * intersection_count
    capacity = (entry_count + tile_count - 1) // tile_count + 1
    buffer_rows = tile_count * capacity
    flat_dest = intersections.reshape(entry_count)
    onehot = (flat_dest[:, None] == jnp.arange(tile_count, dtype=jnp.int32)[None, :]).astype(
        jnp.int32
    )
    slot_rank = jnp.sum((jnp.cumsum(onehot, 0) - onehot) * onehot, 1)
    slot_index = flat_dest * capacity + slot_rank
    raw_planes = jnp.repeat(planes, intersection_count, axis=0)
    matrices = jnp.stack([row_resample, col_resample], 2).reshape(entry_count, 2, pixel_count)
    raw_out = (
        jnp.zeros((buffer_rows, plane_count, pixel_count), jnp.bfloat16)
        .at[slot_index]
        .set(raw_planes)
    )
    matrix_out = jnp.zeros((buffer_rows, 2, pixel_count), jnp.bfloat16).at[slot_index].set(matrices)
    raw_in, matrix_in = (
        lax.all_to_all(raw_out, "tile", split_axis=0, concat_axis=0, tiled=True),
        lax.all_to_all(matrix_out, "tile", split_axis=0, concat_axis=0, tiled=True),
    )
    matrix_in = matrix_in.reshape(buffer_rows, 2, side_cells, side_cells)
    incoming = reproject(
        raw_in.reshape(buffer_rows, plane_count, side_cells, side_cells),
        matrix_in[:, 0],
        matrix_in[:, 1],
    )
    incoming = incoming.reshape(buffer_rows, plane_count, pixel_count)
    estimate = huber_merge(incoming[:, :group_bands], incoming[:, group_bands])
    field = estimate.reshape(group_bands, side_cells, side_cells)
    first_col = lax.axis_index("tile") * side_cells
    total_cols = tile_count * side_cells
    for repeat in range(SMOOTH):
        extended = extended_2(field, (("tile", 2),), 1)
        field = smooth_step(extended, first_col - 1, total_cols)
    return field.reshape(group_bands, pixel_count)


def solution(mesh):
    return jax.shard_map(
        per_device,
        mesh=mesh,
        in_specs=(
            P("tile", "band", None),
            P("tile", None),
            P("tile"),
            P("tile", None),
            P("tile", None, None),
            P("tile", None, None),
            P(),
            P(),
            P(),
        ),
        out_specs=P("band", "tile"),
        check_vma=False,
    )
```

profile of v0, /device:TPU:8, one launch (start us, length us, event | category | flops | bytes accessed | tf_op | source)
XLA Modules:
  0.0 474.6 jit_solution(6735166915798410247)
XLA Ops:
  0.0 6.5 %copy.57 = bf16[16,4,4096]{0,1,2:T(4,128)(2,1)} copy(bf16[16,4,4096]{2,1,0:T(4,128)(2,1)} %param.11) | data formatting | bytes 1048576 | tf_op args[0]
  6.5 6.5 %reshape.136 = bf16[4,2,32768]{2,1,0:T(2,128)(2,1)} reshape(bf16[4096,4,16]{2,1,0:T(4,128)(2,1)} %bitcast.84) | data formatting | bytes 1048576
  13.0 4.3 all-to-all-start
  19.9 2.4 pad_maximum_fusion.1
  22.3 3.4 broadcast_in_dim.40
  25.8 8.2 %scatter_fusion.1 = bf16[128,2,4096]{2,1,0:T(2,128)(2,1)} fusion(bf16[128,2,4096]{2,1,0:T(2,128)(2,1)} %broadcast_in_dim.40, s32[64]{0:T(128)S(1)} %fusion.59, bf16[64,2,4096]{2,1,0:T(2,128)(2,1)S(1)} %pad_maximum_fusion.1), kind=kCustom, calls=%fused_computation.1 | custom fusion | bytes 3145984 | tf_op jit(solution)/shard_map/scatter | solution.py:124
  34.0 12.1 %all-to-all-start.2 = ((bf16[128,2,4096]{2,1,0:T(2,128)(2,1)}), bf16[128,2,4096]{2,1,0:T(2,128)(2,1)S(1)}, u32[]{:S(2)}, u32[]{:S(2)}) async-start(bf16[128,2,4096]{2,1,0:T(2,128)(2,1)} %scatter_fusion.1), calls=%async_computation.2 | async-start | bytes 4194304 | tf_op jit(solution)/shard_map/all_to_all | solution.py:127
  46.1 5.4 %reshape.137 = bf16[4096,4,16]{2,1,0:T(4,128)(2,1)} reshape(bf16[4,2,32768]{2,1,0:T(2,128)(2,1)} %all-to-all-done) | data formatting | bytes 1048576
  51.5 6.1 %copy.58 = bf16[16,4,4,1024]{3,2,1,0:T(4,128)(2,1)S(1)} copy(bf16[16,4,4,1024]{0,2,3,1:T(4,128)(2,1)} %bitcast.83) | data formatting | bytes 1048576 | tf_op jit(solution)/shard_map/all_to_all | solution.py:99
  57.8 74.0 %while.10 = (s32[]{:T(128)}, bf16[16,1024]{1,0:T(8,128)(2,1)S(1)}, bf16[16,16,1024]{2,1,0:T(8,128)(2,1)S(1)}, bf16[16,256]{1,0:T(8,128)(2,1)S(1)}, bf16[2,256,25...) while((s32[]{:T(128)}, bf16[16,1024]{1,0:T(8,128)(2,1)S(1)}, ...), condition=%wide.region_3.4_spmd, body=%wide.region_2.3_spmd.sunk | while | flops 281285632 | bytes 1384577 | solution.py:46
  59.3 1.6 fusion.80
  63.9 1.6 fusion.80
  68.6 1.6 fusion.80
  77.8 1.6 fusion.80
  82.4 1.6 fusion.80
  87.0 1.6 fusion.80
  91.7 1.6 fusion.80
  96.3 1.6 fusion.80
  100.9 1.6 fusion.80
  119.4 1.6 fusion.80
  124.0 1.6 fusion.80
  128.7 1.6 fusion.80
  131.7 12.8 %all_gather.3 = bf16[16,4096]{1,0:T(8,128)(2,1)S(1)} all-gather(bf16[16,1024]{1,0:T(8,128)(2,1)S(1)} %get-tuple-element.47), channel_id=1, replica_groups=mesh['band'=4,'tile'=64] {'band'}, dimensions={1}, use_global_device_ids=true | all-gather | bytes 163840 | tf_op jit(solution)/shard_map/all_gather | solution.py:105
  145.4 2.4 broadcast_in_dim.20.clone
  147.8 4.3 broadcast_in_dim.16
  152.1 11.9 %scatter_fusion = bf16[128,5,4096]{2,1,0:T(8,128)(2,1)} fusion(bf16[128,5,4096]{2,1,0:T(8,128)(2,1)} %broadcast_in_dim.16, s32[64]{0:T(128)S(1)} %fusion.59, bf16[64,5,4096]{2,1,0:T(8,128)(2,1)} %bitcast.82), kind=kCustom, calls=%fused_computation | custom fusion | bytes 7864576 | tf_op jit(solution)/shard_map/scatter | solution.py:122
  164.0 10.5 %all-to-all-start.1 = ((bf16[128,5,4096]{2,1,0:T(8,128)(2,1)}), bf16[128,5,4096]{2,1,0:T(8,128)(2,1)}, u32[]{:S(2)}, u32[]{:S(2)}) async-start(bf16[128,5,4096]{2,1,0:T(8,128)(2,1)} %scatter_fusion), calls=%async_computation.1 | async-start | bytes 16777216 | tf_op jit(solution)/shard_map/all_to_all | solution.py:126
  174.5 4.0 copy.65
  178.6 2.7 fusion.60
  181.3 3.9 copy.75
  185.2 3.8 copy.76
  189.0 169.8 %all-to-all-done.1 = bf16[128,5,4096]{2,1,0:T(8,128)(2,1)} async-done(((bf16[128,5,4096]{2,1,0:T(8,128)(2,1)}), bf16[128,5,4096]{2,1,0:T(8,128)(2,1)}, u32[]{:S(2)}, u32[]{:S(2)}) %all-to-all-start.1) | async-done | bytes 5242912 | tf_op jit(solution)/shard_map/all_to_all | solution.py:126
  358.8 10.6 %copy.62 = bf16[128,5,4096]{0,2,1:T(8,128)(2,1)} copy(bf16[128,5,4096]{2,1,0:T(8,128)(2,1)} %all-to-all-done.1) | data formatting | bytes 10485760 | tf_op jit(solution)/shard_map/all_to_all | solution.py:126
  369.5 15.7 %copy.67 = bf16[128,5,64,64]{3,2,1,0:T(8,128)(2,1)} copy(bf16[128,5,64,64]{0,3,2,1:T(8,128)(2,1)} %bitcast.81) | data formatting | bytes 10485760 | tf_op jit(solution)/shard_map/reshape | solution.py:131
  385.2 12.5 %convert_bitcast_fusion = bf16[128,5,64,64]{2,3,1,0:T(8,128)(2,1)} fusion(bf16[128,5,64,64]{3,2,1,0:T(8,128)(2,1)} %copy.67, bf16[128,1,64,64]{3,2,0,1:T(8,128)(2,1)} %copy.76, bf16[128,1,64,64]{3,2,0,1:T(8,128)(2,1)S(1)} %copy.75), kind=kOutput, calls=%fused_computation.29 | convolution fusion | flops 676331520 | bytes 12582912 | tf_op jit(solution)/shard_map/nij,ncjl->ncil/dot_general | solution.py:53
  397.7 18.1 %copy.70 = bf16[128,5,64,64]{0,3,2,1:T(8,128)(2,1)} copy(bf16[128,5,64,64]{2,3,1,0:T(8,128)(2,1)} %convert_bitcast_fusion) | data formatting | bytes 10485760 | tf_op jit(solution)/shard_map/convert_element_type | solution.py:55
  417.3 1.9 fusion.48
  419.3 2.3 fusion.23
  421.6 7.8 %fusion.47 = (f32[4,4096]{1,0:T(4,128)S(1)}, f32[4,4096]{1,0:T(4,128)S(1)}) fusion(f32[4,4096]{1,0:T(4,128)S(1)} %broadcast_divide_fusion, f32[128,4096]{0,1:T(8,128)S(1)} %get-tuple-element.72, bf16[128,5,4096]{0,2,1:T(8,128)(2,1)S(1)} %bitcast.77), kind=kLoop, calls=%fused_computation.53 | loop fusion | flops 16744448 | bytes 6488064 | tf_op jit(solution)/shard_map/reduce_sum | solution.py:65
  429.4 7.6 %fusion.46 = (f32[4,4096]{1,0:T(4,128)S(1)}, f32[4,4096]{1,0:T(4,128)S(1)}) fusion(f32[4,4096]{1,0:T(4,128)S(1)} %add_divide_fusion.5, f32[128,4096]{0,1:T(8,128)S(1)} %get-tuple-element.72, bf16[128,5,4096]{0,2,1:T(8,128)(2,1)S(1)} %bitcast.78), kind=kLoop, calls=%fused_computation.52 | loop fusion | flops 16744448 | bytes 6488064 | tf_op jit(solution)/shard_map/reduce_sum | solution.py:65
  437.1 7.6 %fusion.45 = (f32[4,4096]{1,0:T(4,128)S(1)}, f32[4,4096]{1,0:T(4,128)S(1)}) fusion(f32[4,4096]{1,0:T(4,128)S(1)} %add_divide_fusion.4, f32[128,4096]{0,1:T(8,128)S(1)} %get-tuple-element.72, bf16[128,5,4096]{0,2,1:T(8,128)(2,1)S(1)} %bitcast.79), kind=kLoop, calls=%fused_computation.51 | loop fusion | flops 16744448 | bytes 6488064 | tf_op jit(solution)/shard_map/reduce_sum | solution.py:65
  444.7 7.6 %fusion.44 = (f32[4,4096]{1,0:T(4,128)S(1)}, f32[4,4096]{1,0:T(4,128)S(1)}) fusion(f32[4,4096]{1,0:T(4,128)S(1)} %add_divide_fusion.3, f32[128,4096]{0,1:T(8,128)S(1)} %get-tuple-element.72, bf16[128,5,4096]{0,2,1:T(8,128)(2,1)S(1)} %bitcast.80), kind=kLoop, calls=%fused_computation.50 | loop fusion | flops 16744448 | bytes 6488064 | tf_op jit(solution)/shard_map/reduce_sum | solution.py:65
  452.6 1.9 collective-permute-start
  454.5 3.3 collective-permute-start.1
  457.8 5.1 %collective-permute-done.1 = f32[4,64,1]{2,1,0:T(8,128)S(1)} collective-permute-done((f32[4,64,1]{2,1,0:T(8,128)S(1)}, f32[4,64,1]{2,1,0:T(8,128)S(1)}, u32[]{:S(2)}, u32[]{:S(2)}) %collective-permute-start.1) | collective-permute-done | bytes 1056 | tf_op jit(solution)/shard_map/ppermute | solution.py:19
  463.3 1.9 collective-permute-start.2
  465.2 2.4 collective-permute-start.3
  467.7 5.9 %collective-permute-done.3 = f32[4,64,1]{2,1,0:T(8,128)S(1)} collective-permute-done((f32[4,64,1]{2,1,0:T(8,128)S(1)}, f32[4,64,1]{2,1,0:T(8,128)S(1)}, u32[]{:S(2)}, u32[]{:S(2)}) %collective-permute-start.3) | collective-permute-done | bytes 1056 | tf_op jit(solution)/shard_map/ppermute | solution.py:19
  (177 shorter events, 61.0 us)
Async XLA Ops:
  0.0 17.3 %copy-start.4 = (s32[16,4]{0,1:T(4,128)S(1)}, s32[16,4]{0,1:T(4,128)}, u32[]{:S(2)}) copy-start(s32[16,4]{0,1:T(4,128)} %param.14) | copy-start | bytes 772
  0.0 17.4 %copy-start.5 = (s32[16,64]{1,0:T(8,128)S(1)}, s32[16,64]{1,0:T(8,128)}, u32[]{:S(2)}) copy-start(s32[16,64]{1,0:T(8,128)} %param.12) | copy-start | bytes 12292
  0.0 18.3 %copy-start.2 = (bf16[16,4,4096]{2,1,0:T(4,128)(2,1)S(1)}, bf16[16,4,4096]{2,1,0:T(4,128)(2,1)}, u32[]{:S(2)}) copy-start(bf16[16,4,4096]{2,1,0:T(4,128)(2,1)} %param.15) | copy-start | bytes 1572868
  0.0 19.1 %copy-start.3 = (bf16[16,4,4096]{2,1,0:T(4,128)(2,1)S(1)}, bf16[16,4,4096]{2,1,0:T(4,128)(2,1)}, u32[]{:S(2)}) copy-start(bf16[16,4,4096]{2,1,0:T(4,128)(2,1)} %param.16) | copy-start | bytes 1572868
  6.5 27.5 %copy-start.8 = (s32[16]{0:T(128)S(1)}, s32[16]{0:T(128)}, u32[]{:S(2)}) copy-start(s32[16]{0:T(128)} %param.13) | copy-start | bytes 196
  13.0 21.0 %all-to-all-start = ((bf16[4,2,32768]{2,1,0:T(2,128)(2,1)}), bf16[4,2,32768]{2,1,0:T(2,128)(2,1)}, u32[]{:S(2)}, u32[]{:S(2)}) async-start(bf16[4,2,32768]{2,1,0:T(2,128)(2,1)} %reshape.136), calls=%async_computation | async-start | bytes 1048576 | tf_op jit(solution)/shard_map/all_to_all | solution.py:99
  25.8 32.0 %copy-start.6 = (bf16[2,256,256]{2,1,0:T(8,128)(2,1)S(1)}, bf16[2,256,256]{2,1,0:T(8,128)(2,1)}, u32[]{:S(2)}) copy-start(bf16[2,256,256]{2,1,0:T(8,128)(2,1)} %param.18) | copy-start | bytes 786436
  25.8 32.0 %copy-start.7 = (bf16[16,256]{1,0:T(8,128)(2,1)S(1)}, bf16[16,256]{1,0:T(8,128)(2,1)}, u32[]{:S(2)}) copy-start(bf16[16,256]{1,0:T(8,128)(2,1)} %param.17) | copy-start | bytes 24580
  25.8 32.0 %copy-start.9 = (bf16[256]{0:T(256)(128)(2,1)S(1)}, bf16[256]{0:T(256)(128)(2,1)}, u32[]{:S(2)}) copy-start(bf16[256]{0:T(256)(128)(2,1)} %param.19) | copy-start | bytes 1540
  34.0 130.0 %all-to-all-start.2 = ((bf16[128,2,4096]{2,1,0:T(2,128)(2,1)}), bf16[128,2,4096]{2,1,0:T(2,128)(2,1)S(1)}, u32[]{:S(2)}, u32[]{:S(2)}) async-start(bf16[128,2,4096]{2,1,0:T(2,128)(2,1)} %scatter_fusion.1), calls=%async_computation.2 | async-start | bytes 4194304 | tf_op jit(solution)/shard_map/all_to_all | solution.py:127
  57.7 87.1 %copy-start.1 = (bf16[16,4,4096]{2,1,0:T(4,128)(2,1)S(1)}, bf16[16,4,4096]{2,1,0:T(4,128)(2,1)}, u32[]{:S(2)}) copy-start(bf16[16,4,4096]{2,1,0:T(4,128)(2,1)} %param.11) | copy-start | bytes 1572868
  164.0 194.8 %all-to-all-start.1 = ((bf16[128,5,4096]{2,1,0:T(8,128)(2,1)}), bf16[128,5,4096]{2,1,0:T(8,128)(2,1)}, u32[]{:S(2)}, u32[]{:S(2)}) async-start(bf16[128,5,4096]{2,1,0:T(8,128)(2,1)} %scatter_fusion), calls=%async_computation.1 | async-start | bytes 16777216 | tf_op jit(solution)/shard_map/all_to_all | solution.py:126
  415.8 3.4 copy-start
  452.6 5.3 %collective-permute-start = (f32[4,64,1]{2,1,0:T(8,128)S(1)}, f32[4,64,1]{2,1,0:T(8,128)S(1)}, u32[]{:S(2)}, u32[]{:S(2)}) collective-permute-start(f32[4,64,1]{2,1,0:T(8,128)S(1)} %get-tuple-element.78), channel_id=1, source_target_pairs={{1,0},{2,1},{3,2},{4,3},{5,4},{6,5},{7,6},{8,7},{9,8},{10,9},{11,1... | collective-permute-start | bytes 3080 | tf_op jit(solution)/shard_map/ppermute | solution.py:22
  454.5 8.4 %collective-permute-start.1 = (f32[4,64,1]{2,1,0:T(8,128)S(1)}, f32[4,64,1]{2,1,0:T(8,128)S(1)}, u32[]{:S(2)}, u32[]{:S(2)}) collective-permute-start(f32[4,64,1]{2,1,0:T(8,128)S(1)} %get-tuple-element.79), channel_id=1, source_target_pairs={{0,1},{1,2},{2,3},{3,4},{4,5},{5,6},{6,7},{7,8},{8,9},{9,10},{10,1... | collective-permute-start | bytes 3080 | tf_op jit(solution)/shard_map/ppermute | solution.py:19
  463.3 4.4 collective-permute-start.2
  465.2 8.4 %collective-permute-start.3 = (f32[4,64,1]{2,1,0:T(8,128)S(1)}, f32[4,64,1]{2,1,0:T(8,128)S(1)}, u32[]{:S(2)}, u32[]{:S(2)}) collective-permute-start(f32[4,64,1]{2,1,0:T(8,128)S(1)} %get-tuple-element.77), channel_id=1, source_target_pairs={{0,1},{1,2},{2,3},{3,4},{4,5},{5,6},{6,7},{7,8},{8,9},{9,10},{10,1... | collective-permute-start | bytes 3080 | tf_op jit(solution)/shard_map/ppermute | solution.py:19
where the time goes:
time: 477 us; the launch traced here: 475 us
  waiting for transfers between devices  181 us (38%)
  local copies, waits for them, and re-layouts  129 us (27%)
  matrix products  62.6 us (13%)
  other arithmetic  51.6 us (11%)
  starting transfers between devices  36.4 us (8%)
  blocking collectives  12.8 us (3%)
    all_to_all x1, waiting for transfers between devices, per_device(): lax.all_to_all(raw_out, 'tile', split_axis=0, concat_axis=0, tiled=True)  170 us
    reduce_sum x4, other arithmetic, huber_merge(): jnp.sum(huber_w, 0) + prior_weight  30.6 us
    unnamed x26, local copies, waits for them, and re-layouts  26.2 us
    dot_general x16, matrix products, one_scene(): logits = jnp.dot(hidden, w_out, preferred_element_type=jnp.float32)  25.4 us
    dot_general x16, matrix products, one_scene(): jnp.dot(hidden, w_hidden[repeat], preferred_element_type=jnp.float32)  24.6 us
    convert_element_type x1, local copies, waits for them, and re-layouts, reproject(): return jnp.einsum('nij,ncjl->ncil', rows_matrix, half_done, preferred_ele...  18.1 us
    reshape x1, local copies, waits for them, and re-layouts, per_device(): raw_in.reshape(buffer_rows, plane_count, side_cells, side_cells)  15.7 us
    all_gather x1, blocking collectives, per_device(): weights = lax.all_gather(partial_weights, 'band', axis=1, tiled=True)  12.8 us
  transfers between devices with their start and end apart: 7, of which 3 were waited for; matrix products, arithmetic and copies ran while one was open for 29% of the time, Pallas kernels for 0%

commit v1 on v0

--- a/solution.py
+++ b/solution.py
@@ -96,7 +96,10 @@
     tile_count = lax.axis_size("tile")
     band_count = lax.axis_size("band")
     recency = jnp.exp(1.4 * scene_order.astype(jnp.float32) / (scenes * tile_count) - 0.7)
-    by_rows = lax.all_to_all(granules, "band", split_axis=2, concat_axis=1, tiled=True)
+    by_rows = jnp.concatenate(
+        lax.all_to_all(jnp.stack(jnp.split(granules, lax.axis_size("band"), axis=2)), "band", 0, 0),
+        axis=1,
+    )
     row_count = side_cells // band_count
     valid_here = lax.dynamic_slice_in_dim(
         valid_rows, lax.axis_index("band") * row_count, row_count, 1

time: 477 us -> 462 us (0.969)
  local copies, waits for them, and re-layouts: 129 us -> 111 us
    unnamed x26 -> x15, local copies, waits for them, and re-layouts: 26.2 us -> 8.52 us
    all_to_all x2 -> x0, local copies, waits for them, and re-layouts: 6.2 us -> none  [per_device(): lax.all_to_all(granules, 'band', split_axis=2, concat_axis=1, tiled=True)]
  transfers between devices with their start and end apart: 7 -> 7, of which waited for: 3 -> 3; matrix products, arithmetic and copies ran while one was open for 29% -> 28% of each run, Pallas kernels for 0% -> 0%
where the time goes in v1:
time: 462 us; the launch traced here: 459 us
  waiting for transfers between devices  181 us (39%)
  local copies, waits for them, and re-layouts  111 us (24%)
  matrix products  62.5 us (14%)
  other arithmetic  54.2 us (12%)
  starting transfers between devices  36.4 us (8%)
  blocking collectives  12.8 us (3%)
    all_to_all x1, waiting for transfers between devices, per_device(): lax.all_to_all(raw_out, 'tile', split_axis=0, concat_axis=0, tiled=True)  170 us
    reduce_sum x4, other arithmetic, huber_merge(): jnp.sum(huber_w, 0) + prior_weight  30.6 us
    dot_general x16, matrix products, one_scene(): logits = jnp.dot(hidden, w_out, preferred_element_type=jnp.float32)  25.4 us
    dot_general x16, matrix products, one_scene(): jnp.dot(hidden, w_hidden[repeat], preferred_element_type=jnp.float32)  24.6 us
    convert_element_type x1, local copies, waits for them, and re-layouts, reproject(): return jnp.einsum('nij,ncjl->ncil', rows_matrix, half_done, preferred_ele...  18.1 us
    reshape x1, local copies, waits for them, and re-layouts, per_device(): raw_in.reshape(buffer_rows, plane_count, side_cells, side_cells)  15.7 us
    all_gather x1, blocking collectives, per_device(): weights = lax.all_gather(partial_weights, 'band', axis=1, tiled=True)  12.8 us
    dot_general x1, matrix products, reproject(): jnp.einsum('nij,ncjl->ncil', rows_matrix, half_done, preferred_element_ty...  12.5 us
  transfers between devices with their start and end apart: 7, of which 3 were waited for; matrix products, arithmetic and copies ran while one was open for 28% of the time, Pallas kernels for 0%

profile of v1, /device:TPU:8, one launch (start us, length us, event | category | flops | bytes accessed | tf_op | source)
XLA Modules:
  0.0 459.3 jit_solution(5959264171993118642)
XLA Ops:
  2.6 4.3 all-to-all-start
  9.9 2.4 stack.32
  12.4 2.4 stack.33
  14.8 2.4 pad_maximum_fusion.1
  17.3 3.4 broadcast_in_dim.40
  20.7 8.2 %scatter_fusion.1 = bf16[128,2,4096]{2,1,0:T(2,128)(2,1)} fusion(bf16[128,2,4096]{2,1,0:T(2,128)(2,1)} %broadcast_in_dim.40, s32[64]{0:T(128)S(1)} %fusion.59, bf16[64,2,4096]{2,1,0:T(2,128)(2,1)S(1)} %pad_maximum_fusion.1), kind=kCustom, calls=%fused_computation.1 | custom fusion | bytes 3145984 | tf_op jit(solution)/shard_map/scatter | solution.py:127
  28.9 12.1 %all-to-all-start.2 = ((bf16[128,2,4096]{2,1,0:T(2,128)(2,1)}), bf16[128,2,4096]{2,1,0:T(2,128)(2,1)S(1)}, u32[]{:S(2)}, u32[]{:S(2)}) async-start(bf16[128,2,4096]{2,1,0:T(2,128)(2,1)} %scatter_fusion.1), calls=%async_computation.2 | async-start | bytes 4194304 | tf_op jit(solution)/shard_map/all_to_all | solution.py:130
  42.5 73.9 %while.10 = (s32[]{:T(128)}, bf16[16,1024]{1,0:T(8,128)(2,1)S(1)}, bf16[16,16,1024]{2,1,0:T(8,128)(2,1)S(1)}, bf16[16,256]{1,0:T(8,128)(2,1)S(1)}, bf16[2,256,25...) while((s32[]{:T(128)}, bf16[16,1024]{1,0:T(8,128)(2,1)S(1)}, ...), condition=%wide.region_3.4_spmd, body=%wide.region_2.3_spmd.sunk | while | flops 281285632 | bytes 1384577 | solution.py:46
  44.1 1.6 fusion.80
  48.7 1.6 fusion.80
  53.3 1.6 fusion.80
  57.9 1.6 fusion.80
  62.6 1.6 fusion.80
  67.2 1.6 fusion.80
  71.8 1.6 fusion.80
  76.4 1.6 fusion.80
  85.7 1.6 fusion.80
  90.3 1.6 fusion.80
  94.9 1.6 fusion.80
  99.5 1.6 fusion.80
  104.1 1.6 fusion.80
  113.4 1.6 fusion.80
  116.4 12.8 %all_gather.3 = bf16[16,4096]{1,0:T(8,128)(2,1)S(1)} all-gather(bf16[16,1024]{1,0:T(8,128)(2,1)S(1)} %get-tuple-element.47), channel_id=1, replica_groups=mesh['band'=4,'tile'=64] {'band'}, dimensions={1}, use_global_device_ids=true | all-gather | bytes 163840 | tf_op jit(solution)/shard_map/all_gather | solution.py:108
  130.1 2.4 broadcast_in_dim.20.clone
  132.5 4.3 broadcast_in_dim.16
  136.8 11.9 %scatter_fusion = bf16[128,5,4096]{2,1,0:T(8,128)(2,1)} fusion(bf16[128,5,4096]{2,1,0:T(8,128)(2,1)} %broadcast_in_dim.16, s32[64]{0:T(128)S(1)} %fusion.59, bf16[64,5,4096]{2,1,0:T(8,128)(2,1)} %bitcast.86), kind=kCustom, calls=%fused_computation | custom fusion | bytes 7864576 | tf_op jit(solution)/shard_map/scatter | solution.py:125
  148.7 10.5 %all-to-all-start.1 = ((bf16[128,5,4096]{2,1,0:T(8,128)(2,1)}), bf16[128,5,4096]{2,1,0:T(8,128)(2,1)}, u32[]{:S(2)}, u32[]{:S(2)}) async-start(bf16[128,5,4096]{2,1,0:T(8,128)(2,1)} %scatter_fusion), calls=%async_computation.1 | async-start | bytes 16777216 | tf_op jit(solution)/shard_map/all_to_all | solution.py:129
  159.2 4.0 copy.33
  163.3 2.7 fusion.60
  166.0 3.9 copy.43
  169.9 3.8 copy.44
  173.7 169.8 %all-to-all-done.1 = bf16[128,5,4096]{2,1,0:T(8,128)(2,1)} async-done(((bf16[128,5,4096]{2,1,0:T(8,128)(2,1)}), bf16[128,5,4096]{2,1,0:T(8,128)(2,1)}, u32[]{:S(2)}, u32[]{:S(2)}) %all-to-all-start.1) | async-done | bytes 5242912 | tf_op jit(solution)/shard_map/all_to_all | solution.py:129
  343.6 10.6 %copy.30 = bf16[128,5,4096]{0,2,1:T(8,128)(2,1)} copy(bf16[128,5,4096]{2,1,0:T(8,128)(2,1)} %all-to-all-done.1) | data formatting | bytes 10485760 | tf_op jit(solution)/shard_map/all_to_all | solution.py:129
  354.2 15.7 %copy.35 = bf16[128,5,64,64]{3,2,1,0:T(8,128)(2,1)} copy(bf16[128,5,64,64]{0,3,2,1:T(8,128)(2,1)} %bitcast.85) | data formatting | bytes 10485760 | tf_op jit(solution)/shard_map/reshape | solution.py:134
  369.9 12.5 %convert_bitcast_fusion = bf16[128,5,64,64]{2,3,1,0:T(8,128)(2,1)} fusion(bf16[128,5,64,64]{3,2,1,0:T(8,128)(2,1)} %copy.35, bf16[128,1,64,64]{3,2,0,1:T(8,128)(2,1)} %copy.44, bf16[128,1,64,64]{3,2,0,1:T(8,128)(2,1)S(1)} %copy.43), kind=kOutput, calls=%fused_computation.29 | convolution fusion | flops 676331520 | bytes 12582912 | tf_op jit(solution)/shard_map/nij,ncjl->ncil/dot_general | solution.py:53
  382.4 18.1 %copy.38 = bf16[128,5,64,64]{0,3,2,1:T(8,128)(2,1)} copy(bf16[128,5,64,64]{2,3,1,0:T(8,128)(2,1)} %convert_bitcast_fusion) | data formatting | bytes 10485760 | tf_op jit(solution)/shard_map/convert_element_type | solution.py:55
  402.0 1.9 fusion.48
  404.0 2.3 fusion.23
  406.3 7.8 %fusion.47 = (f32[4,4096]{1,0:T(4,128)S(1)}, f32[4,4096]{1,0:T(4,128)S(1)}) fusion(f32[4,4096]{1,0:T(4,128)S(1)} %broadcast_divide_fusion, f32[128,4096]{0,1:T(8,128)S(1)} %get-tuple-element.72, bf16[128,5,4096]{0,2,1:T(8,128)(2,1)S(1)} %bitcast.81), kind=kLoop, calls=%fused_computation.53 | loop fusion | flops 16744448 | bytes 6488064 | tf_op jit(solution)/shard_map/reduce_sum | solution.py:65
  414.1 7.6 %fusion.46 = (f32[4,4096]{1,0:T(4,128)S(1)}, f32[4,4096]{1,0:T(4,128)S(1)}) fusion(f32[4,4096]{1,0:T(4,128)S(1)} %add_divide_fusion.5, f32[128,4096]{0,1:T(8,128)S(1)} %get-tuple-element.72, bf16[128,5,4096]{0,2,1:T(8,128)(2,1)S(1)} %bitcast.82), kind=kLoop, calls=%fused_computation.52 | loop fusion | flops 16744448 | bytes 6488064 | tf_op jit(solution)/shard_map/reduce_sum | solution.py:65
  421.8 7.6 %fusion.45 = (f32[4,4096]{1,0:T(4,128)S(1)}, f32[4,4096]{1,0:T(4,128)S(1)}) fusion(f32[4,4096]{1,0:T(4,128)S(1)} %add_divide_fusion.4, f32[128,4096]{0,1:T(8,128)S(1)} %get-tuple-element.72, bf16[128,5,4096]{0,2,1:T(8,128)(2,1)S(1)} %bitcast.83), kind=kLoop, calls=%fused_computation.51 | loop fusion | flops 16744448 | bytes 6488064 | tf_op jit(solution)/shard_map/reduce_sum | solution.py:65
  429.4 7.6 %fusion.44 = (f32[4,4096]{1,0:T(4,128)S(1)}, f32[4,4096]{1,0:T(4,128)S(1)}) fusion(f32[4,4096]{1,0:T(4,128)S(1)} %add_divide_fusion.3, f32[128,4096]{0,1:T(8,128)S(1)} %get-tuple-element.72, bf16[128,5,4096]{0,2,1:T(8,128)(2,1)S(1)} %bitcast.84), kind=kLoop, calls=%fused_computation.50 | loop fusion | flops 16744448 | bytes 6488064 | tf_op jit(solution)/shard_map/reduce_sum | solution.py:65
  437.3 1.9 collective-permute-start
  439.2 3.3 collective-permute-start.1
  442.6 5.1 %collective-permute-done.1 = f32[4,64,1]{2,1,0:T(8,128)S(1)} collective-permute-done((f32[4,64,1]{2,1,0:T(8,128)S(1)}, f32[4,64,1]{2,1,0:T(8,128)S(1)}, u32[]{:S(2)}, u32[]{:S(2)}) %collective-permute-start.1) | collective-permute-done | bytes 1056 | tf_op jit(solution)/shard_map/ppermute | solution.py:19
  448.0 1.9 collective-permute-start.2
  449.9 2.4 collective-permute-start.3
  452.4 5.9 %collective-permute-done.3 = f32[4,64,1]{2,1,0:T(8,128)S(1)} collective-permute-done((f32[4,64,1]{2,1,0:T(8,128)S(1)}, f32[4,64,1]{2,1,0:T(8,128)S(1)}, u32[]{:S(2)}, u32[]{:S(2)}) %collective-permute-start.3) | collective-permute-done | bytes 1056 | tf_op jit(solution)/shard_map/ppermute | solution.py:19
  (168 shorter events, 62.1 us)
Async XLA Ops:
  0.0 28.9 %copy-start.4 = (s32[16]{0:T(128)S(1)}, s32[16]{0:T(128)}, u32[]{:S(2)}) copy-start(s32[16]{0:T(128)} %param.13) | copy-start | bytes 196
  2.6 26.3 %all-to-all-start = ((bf16[4,16,4,1024]{3,2,1,0:T(4,128)(2,1)}), bf16[4,16,4,1024]{3,2,1,0:T(4,128)(2,1)}, u32[]{:S(2)}, u32[]{:S(2)}) async-start(bf16[4,16,4,1024]{3,2,1,0:T(4,128)(2,1)} %pad_maximum_fusion.2), calls=%async_computation | async-start | bytes 1048576 | tf_op jit(solution)/shard_map/all_to_all | solution.py:100
  12.3 30.2 %copy-start.2 = (bf16[2,256,256]{2,1,0:T(8,128)(2,1)S(1)}, bf16[2,256,256]{2,1,0:T(8,128)(2,1)}, u32[]{:S(2)}) copy-start(bf16[2,256,256]{2,1,0:T(8,128)(2,1)} %param.18) | copy-start | bytes 786436
  12.3 30.2 %copy-start.3 = (bf16[16,256]{1,0:T(8,128)(2,1)S(1)}, bf16[16,256]{1,0:T(8,128)(2,1)}, u32[]{:S(2)}) copy-start(bf16[16,256]{1,0:T(8,128)(2,1)} %param.17) | copy-start | bytes 24580
  12.4 30.2 %copy-start.5 = (bf16[256]{0:T(256)(128)(2,1)S(1)}, bf16[256]{0:T(256)(128)(2,1)}, u32[]{:S(2)}) copy-start(bf16[256]{0:T(256)(128)(2,1)} %param.19) | copy-start | bytes 1540
  28.9 119.8 %all-to-all-start.2 = ((bf16[128,2,4096]{2,1,0:T(2,128)(2,1)}), bf16[128,2,4096]{2,1,0:T(2,128)(2,1)S(1)}, u32[]{:S(2)}, u32[]{:S(2)}) async-start(bf16[128,2,4096]{2,1,0:T(2,128)(2,1)} %scatter_fusion.1), calls=%async_computation.2 | async-start | bytes 4194304 | tf_op jit(solution)/shard_map/all_to_all | solution.py:130
  42.5 87.0 %copy-start.1 = (bf16[16,4,4096]{2,1,0:T(4,128)(2,1)S(1)}, bf16[16,4,4096]{2,1,0:T(4,128)(2,1)}, u32[]{:S(2)}) copy-start(bf16[16,4,4096]{2,1,0:T(4,128)(2,1)} %param.11) | copy-start | bytes 1572868
  148.7 194.8 %all-to-all-start.1 = ((bf16[128,5,4096]{2,1,0:T(8,128)(2,1)}), bf16[128,5,4096]{2,1,0:T(8,128)(2,1)}, u32[]{:S(2)}, u32[]{:S(2)}) async-start(bf16[128,5,4096]{2,1,0:T(8,128)(2,1)} %scatter_fusion), calls=%async_computation.1 | async-start | bytes 16777216 | tf_op jit(solution)/shard_map/all_to_all | solution.py:129
  400.5 3.4 copy-start
  437.3 5.3 %collective-permute-start = (f32[4,64,1]{2,1,0:T(8,128)S(1)}, f32[4,64,1]{2,1,0:T(8,128)S(1)}, u32[]{:S(2)}, u32[]{:S(2)}) collective-permute-start(f32[4,64,1]{2,1,0:T(8,128)S(1)} %get-tuple-element.82), channel_id=1, source_target_pairs={{1,0},{2,1},{3,2},{4,3},{5,4},{6,5},{7,6},{8,7},{9,8},{10,9},{11,1... | collective-permute-start | bytes 3080 | tf_op jit(solution)/shard_map/ppermute | solution.py:22
  439.2 8.4 %collective-permute-start.1 = (f32[4,64,1]{2,1,0:T(8,128)S(1)}, f32[4,64,1]{2,1,0:T(8,128)S(1)}, u32[]{:S(2)}, u32[]{:S(2)}) collective-permute-start(f32[4,64,1]{2,1,0:T(8,128)S(1)} %get-tuple-element.83), channel_id=1, source_target_pairs={{0,1},{1,2},{2,3},{3,4},{4,5},{5,6},{6,7},{7,8},{8,9},{9,10},{10,1... | collective-permute-start | bytes 3080 | tf_op jit(solution)/shard_map/ppermute | solution.py:19
  448.0 4.4 collective-permute-start.2
  449.9 8.4 %collective-permute-start.3 = (f32[4,64,1]{2,1,0:T(8,128)S(1)}, f32[4,64,1]{2,1,0:T(8,128)S(1)}, u32[]{:S(2)}, u32[]{:S(2)}) collective-permute-start(f32[4,64,1]{2,1,0:T(8,128)S(1)} %get-tuple-element.81), channel_id=1, source_target_pairs={{0,1},{1,2},{2,3},{3,4},{4,5},{5,6},{6,7},{7,8},{8,9},{9,10},{10,1... | collective-permute-start | bytes 3080 | tf_op jit(solution)/shard_map/ppermute | solution.py:19
